TPU v7x, 32 devices: a whole 2x2x4 slice. The times are simulated.
32 devices in a mesh: seq: 8 (over z, y), head: 4 (over x, core).
Axes of the slice: x: 2, y: 2, z: 4, core: 2. Of those that a mesh axis runs over, the one named last changes fastest.
Arguments:
- queries: bfloat16 [8, 1024, 128], P('head', 'seq')
- keys: bfloat16 [8, 1024, 128], P('head', 'seq')
- values: bfloat16 [8, 1024, 128], P('head', 'seq'), may hold values from -6 to 6
- grad_out: bfloat16 [8, 1024, 128], P('head', 'seq'), may hold values from -96 to 96
- rand_ids: int32 [8, 16, 3], P('head', 'seq'), may hold values from 0 to 15, as said below
- global_ids: int32 [2], replicated, may hold values from 0 to 15
Outputs:
- grad_queries: bfloat16 [8, 1024, 128], P('head', 'seq')
- grad_keys: bfloat16 [8, 1024, 128], P('head', 'seq')
- grad_values: bfloat16 [8, 1024, 128], P('head', 'seq')
Inputs may be any that keep to these rules, and one draw needn't show every extreme that they name: `rand_ids`: for each head and slot j there is one number M, 0 <= M < 8, such that every query block b names in slot j a block e * 2 + l with e = (b // 2) XOR M and 0 <= l < 2.
All inputs are finite; a program needn't handle non-finite values.
Results may differ from a plain program's by a relative error of at most 0.03.
Values may be sent and summed in bfloat16 or wider, within the bound.
No kernel may reach another device: no remote copies, remote signals or barrier semaphores. Data moves between devices by JAX's collectives and lax.ppermute only.
A program may use at most 64 MiB of HBM per device.

v0:
```python
import math
import jax
import jax.numpy as jnp
from jax import lax
from jax.sharding import PartitionSpec as P


def with_halo(value, sides, width):
    for axis, dim in sides:
        peers, length = (lax.axis_size(axis), value.shape[dim])
        up = [(i, (i + 1) % peers) for i in range(peers - 1)]
        down = [(j, i) for i, j in up]
        last = lax.slice_in_dim(value, length - width, length, axis=dim)
        initial = lax.slice_in_dim(value, 0, width, axis=dim)
        before = lax.ppermute(last, axis, up)
        after = lax.ppermute(initial, axis, down)
        value = jnp.concatenate([before, value, after], axis=dim)
    return value


def swapped(value, axis, distance):
    mask = 2**distance
    pairs = [(source, source ^ mask) for source in range(lax.axis_size(axis))]
    return lax.ppermute(value, axis, pairs)


def section_list(section_count):
    return list(range(section_count))


def on_device(queries, keys, values, grad_out, rand_ids, global_ids):
    head_count, row_count, head_width = queries.shape
    block_count = rand_ids.shape[1]
    slot_count = rand_ids.shape[2]
    block_rows = row_count // block_count
    global_count = global_ids.shape[0]
    slot_total = 3 + global_count + slot_count
    device = lax.axis_index("seq")
    seq_count = lax.axis_size("seq")
    sections = section_list(seq_count.bit_length() - 1)
    score_scale = 1.0 / math.sqrt(head_width)
    key_vals = jnp.stack([keys, values])
    padded = with_halo(key_vals, (("seq", 2),), block_rows)
    padded_blocks = padded.reshape(2, head_count, block_count + 2, block_rows, head_width)
    window = jnp.stack(
        [
            padded_blocks[:, :, 0:block_count],
            padded_blocks[:, :, 1 : block_count + 1],
            padded_blocks[:, :, 2 : block_count + 2],
        ],
        3,
    )
    key_blocks = key_vals.reshape(2, head_count, block_count, block_rows, head_width)
    global_local = global_ids % block_count
    global_owner = global_ids // block_count
    owned = (global_owner == device).astype(jnp.float32)
    picked = jnp.take(key_blocks, global_local, axis=2).astype(jnp.float32)
    global_sum = lax.psum(picked * owned[None, None, :, None, None], "seq")
    global_kv = global_sum.astype(jnp.bfloat16)
    global_keys = jnp.broadcast_to(
        global_kv[:, :, None], (2, head_count, block_count, global_count, block_rows, head_width)
    )
    xor_masks = jnp.bitwise_xor(rand_ids[:, 0, :] // block_count, device)
    pieces = []
    for slot_index in range(slot_count):
        moving = key_vals
        for bit_index in sections:
            arrived = swapped(moving, "seq", bit_index)
            flag_now = jnp.right_shift(xor_masks[:, slot_index], bit_index) & 1 == 1
            moving = jnp.where(flag_now[None, :, None, None], arrived, moving)
        pieces.append(moving)
    routed = jnp.stack(pieces)
    routed_blocks = routed.reshape(slot_count, 2, head_count, block_count, block_rows, head_width)
    random_local = rand_ids % block_count
    local_onehot = (random_local[..., None] == jnp.arange(block_count, dtype=jnp.int32)).astype(
        jnp.bfloat16
    )
    random_keys = jnp.einsum(
        "hqjl,jchlbd->chqjbd", local_onehot, routed_blocks, preferred_element_type=jnp.float32
    ).astype(jnp.bfloat16)
    all_keys = jnp.concatenate([window, global_keys, random_keys], axis=3)
    key_list = all_keys[0].reshape(head_count, block_count, slot_total * block_rows, head_width)
    value_list = all_keys[1].reshape(head_count, block_count, slot_total * block_rows, head_width)
    block_range = jnp.arange(block_count, dtype=jnp.int32)
    left_valid = jnp.logical_not((block_range == 0) & (device == 0))
    right_valid = jnp.logical_not((block_range == block_count - 1) & (device == seq_count - 1))
    valid = jnp.concatenate(
        [
            left_valid[:, None],
            jnp.ones((block_count, 1), bool),
            right_valid[:, None],
            jnp.ones((block_count, global_count + slot_count), bool),
        ],
        1,
    )
    mask = jnp.repeat(valid, block_rows, axis=1)[None, :, None, :]
    query_blocks = queries.reshape(head_count, block_count, block_rows, head_width)
    grad_blocks = grad_out.reshape(head_count, block_count, block_rows, head_width)
    scores = (
        jnp.einsum("hnqd,hnkd->hnqk", query_blocks, key_list, preferred_element_type=jnp.float32)
        * score_scale
    )
    row_max = jnp.max(jnp.where(mask, scores, -1e30), -1)
    total = jnp.sum(jnp.where(mask, jnp.exp(scores - row_max[..., None]), 0.0), -1)
    log_total = row_max + jnp.log(total)
    probs = jnp.where(mask, jnp.exp(scores - log_total[..., None]), 0.0)
    probs_low = probs.astype(jnp.bfloat16)
    output = jnp.einsum(
        "hnqk,hnkd->hnqd", probs_low, value_list, preferred_element_type=jnp.float32
    )
    row_dot = jnp.sum(grad_blocks.astype(jnp.float32) * output, -1)
    grad_probs = jnp.einsum(
        "hnqd,hnkd->hnqk", grad_blocks, value_list, preferred_element_type=jnp.float32
    )
    scores_low = (probs * (grad_probs - row_dot[..., None])).astype(jnp.bfloat16)
    grad_query = score_scale * jnp.einsum(
        "hnqk,hnkd->hnqd", scores_low, key_list, preferred_element_type=jnp.float32
    )
    key_terms = score_scale * jnp.einsum(
        "hnqk,hnqd->hnkd", scores_low, query_blocks, preferred_element_type=jnp.float32
    )
    value_terms = jnp.einsum(
        "hnqk,hnqd->hnkd", probs_low, grad_blocks, preferred_element_type=jnp.float32
    )
    grads = jnp.stack([key_terms, value_terms]).reshape(
        2, head_count, block_count, slot_total, block_rows, head_width
    )
    no_pad = (0, 0)
    frame_sum = jnp.pad(grads[:, :, :, 0], (no_pad, no_pad, (0, 2), no_pad, no_pad))
    frame_sum = frame_sum + jnp.pad(grads[:, :, :, 1], (no_pad, no_pad, (1, 1), no_pad, no_pad))
    frame_sum = frame_sum + jnp.pad(grads[:, :, :, 2], (no_pad, no_pad, (2, 0), no_pad, no_pad))
    own_grads = frame_sum[:, :, 1 : block_count + 1]
    rim_parts = jnp.concatenate([frame_sum[:, :, 0], frame_sum[:, :, block_count + 1]], axis=2)
    rim_back = with_halo(rim_parts.astype(jnp.bfloat16), (("seq", 2),), block_rows).astype(
        rim_parts.dtype
    )
    own_grads = own_grads.at[:, :, 0].add(rim_back[:, :, 0:block_rows])
    own_grads = own_grads.at[:, :, block_count - 1].add(
        rim_back[:, :, 3 * block_rows : 4 * block_rows]
    )
    global_part = jnp.sum(grads[:, :, :, 3 : 3 + global_count], axis=2)
    global_total = lax.psum(global_part, "seq")
    global_onehot = (
        (global_local[:, None] == block_range[None, :]) & (global_owner == device)[:, None]
    ).astype(jnp.float32)
    own_grads = own_grads + jnp.einsum(
        "gn,chgbd->chnbd", global_onehot, global_total, precision=lax.Precision.HIGHEST
    )
    random_part = grads[:, :, :, 3 + global_count :]
    local_float = (random_local[..., None] == block_range).astype(jnp.float32)
    send_back = jnp.einsum(
        "hqjl,chqjbd->jchlbd", local_float, random_part, precision=lax.Precision.HIGHEST
    )
    send_back = send_back.astype(jnp.bfloat16).reshape(
        slot_count, 2, head_count, row_count, head_width
    )
    pieces = []
    for slot_index in range(slot_count):
        moving = send_back[slot_index]
        for bit_index in sections:
            arrived = swapped(moving, "seq", bit_index)
            flag_now = jnp.right_shift(xor_masks[:, slot_index], bit_index) & 1 == 1
            moving = jnp.where(flag_now[None, :, None, None], arrived, moving)
        pieces.append(moving)
    returned = jnp.stack(pieces)
    returned_sum = jnp.sum(returned.astype(jnp.float32), axis=0).reshape(
        2, head_count, block_count, block_rows, head_width
    )
    own_grads = own_grads + returned_sum
    grad_queries = grad_query.reshape(head_count, row_count, head_width).astype(jnp.bfloat16)
    grad_keys = own_grads[0].reshape(head_count, row_count, head_width).astype(jnp.bfloat16)
    grad_values = own_grads[1].reshape(head_count, row_count, head_width).astype(jnp.bfloat16)
    return (grad_queries, grad_keys, grad_values)


def solution(mesh):
    in_specs = (
        P("head", "seq", None),
        P("head", "seq", None),
        P("head", "seq", None),
        P("head", "seq", None),
        P("head", "seq", None),
        P(),
    )
    out_specs = (P("head", "seq", None), P("head", "seq", None), P("head", "seq", None))
    return jax.shard_map(
        on_device, mesh=mesh, in_specs=in_specs, out_specs=out_specs, check_vma=False
    )
```

profile of v0, /device:TPU:0, one launch (start us, length us, event | category | flops | bytes accessed | tf_op | source)
XLA Modules:
  0.0 174.2 jit_solution(11851105725441294419)
XLA Ops:
  7.2 0.9 fusion.24
  8.1 1.3 collective-permute-start.1
  9.4 5.5 %collective-permute-start = (bf16[2,2,64,128]{3,2,1,0:T(8,128)(2,1)S(1)}, bf16[2,2,64,128]{3,2,1,0:T(8,128)(2,1)S(1)}, u32[]{:S(2)}, u32[]{:S(2)}) collective-permute-start(bf16[2,2,64,128]{3,2,1,0:T(8,128)(2,1)S(1)} %get-tuple-element.60), channel_id=1, source_target_pairs={{0,4},{4,8},{8,12},{12,16},{16,20},{20,24},{24,28},{1,5},{5,9},{9,... | collective-permute-start | bytes 196616 | tf_op jit(solution)/shard_map/ppermute | solution.py:15
  15.0 3.0 %collective-permute-start.2 = (bf16[2,2,128,128]{3,2,1,0:T(8,128)(2,1)S(1)}, bf16[2,2,128,128]{3,2,1,0:T(8,128)(2,1)S(1)}, u32[]{:S(2)}, u32[]{:S(2)}) collective-permute-start(bf16[2,2,128,128]{3,2,1,0:T(8,128)(2,1)S(1)} %pad_maximum_fusion.7), channel_id=1, source_target_pairs={{0,4},{4,0},{8,12},{12,8},{16,20},{20,16},{24,28},{28,24},{1,5},{5... | collective-permute-start | bytes 393224 | tf_op jit(solution)/shard_map/ppermute | solution.py:24
  18.0 0.6 copy-done.5
  18.7 0.6 gather_fusion
  19.4 38.6 %all-reduce.7 = bf16[2,2,2,64,128]{4,3,1,0,2:T(8,128)(2,1)S(1)} all-reduce(f32[2,2,2,64,128]{4,3,1,0,2:T(8,128)S(1)} %multiply_bitcast_fusion), channel_id=1, replica_groups=mesh['seq'=8,'head'=4] {'seq'}, use_global_device_ids=true, to_apply=%region_0.1 | all-reduce | flops 65536 | bytes 393216 | tf_op jit(solution)/shard_map/psum | solution.py:58
  58.0 0.7 slice-done
  59.2 0.3 compare_reduce_fusion.8
  60.4 2.1 %collective-permute-start.5 = (bf16[2,2,128,128]{3,2,1,0:T(8,128)(2,1)S(1)}, bf16[2,2,128,128]{3,2,1,0:T(8,128)(2,1)S(1)}, u32[]{:S(2)}, u32[]{:S(2)}) collective-permute-start(bf16[2,2,128,128]{3,2,1,0:T(8,128)(2,1)S(1)} %get-tuple-element.54), channel_id=1, source_target_pairs={{0,8},{4,12},{8,0},{12,4},{16,24},{20,28},{24,16},{28,20},{1,9},{5... | collective-permute-start | bytes 393224 | tf_op jit(solution)/shard_map/ppermute | solution.py:24
  62.6 4.0 %collective-permute-done.7 = bf16[2,2,128,128]{3,2,1,0:T(8,128)(2,1)S(1)} collective-permute-done((bf16[2,2,128,128]{3,2,1,0:T(8,128)(2,1)S(1)}, bf16[2,2,128,128]{3,2,1,0:T(8,128)(2,1)S(1)}, u32[]{:S(2)}, u32[]{:S(2)}) %collective-permute-start.7) | collective-permute-done | bytes 131104 | tf_op jit(solution)/shard_map/ppermute | solution.py:24
  66.8 2.9 %collective-permute-done.5 = bf16[2,2,128,128]{3,2,1,0:T(8,128)(2,1)S(1)} collective-permute-done((bf16[2,2,128,128]{3,2,1,0:T(8,128)(2,1)S(1)}, bf16[2,2,128,128]{3,2,1,0:T(8,128)(2,1)S(1)}, u32[]{:S(2)}, u32[]{:S(2)}) %collective-permute-start.5) | collective-permute-done | bytes 131104 | tf_op jit(solution)/shard_map/ppermute | solution.py:24
  69.8 1.2 collective-permute-done.3
  71.2 1.7 %collective-permute-start.4 = (bf16[2,2,128,128]{3,2,1,0:T(8,128)(2,1)S(1)}, bf16[2,2,128,128]{3,2,1,0:T(8,128)(2,1)S(1)}, u32[]{:S(2)}, u32[]{:S(2)}) collective-permute-start(bf16[2,2,128,128]{3,2,1,0:T(8,128)(2,1)S(1)} %broadcast_select_fusion.13), channel_id=1, source_target_pairs={{0,16},{4,20},{8,24},{12,28},{16,0},{20,4},{24,8},{28,12},{1,17},{... | collective-permute-start | bytes 393224 | tf_op jit(solution)/shard_map/ppermute | solution.py:24
  72.9 3.4 %collective-permute-done.8 = bf16[2,2,128,128]{3,2,1,0:T(8,128)(2,1)S(1)} collective-permute-done((bf16[2,2,128,128]{3,2,1,0:T(8,128)(2,1)S(1)}, bf16[2,2,128,128]{3,2,1,0:T(8,128)(2,1)S(1)}, u32[]{:S(2)}, u32[]{:S(2)}) %collective-permute-start.8) | collective-permute-done | bytes 131104 | tf_op jit(solution)/shard_map/ppermute | solution.py:24
  76.5 1.7 collective-permute-done.6
  78.4 1.4 collective-permute-done.4
  80.0 0.8 fusion.4
  80.8 1.2 fusion.49
  82.0 0.4 select_reduce_fusion.1
  82.4 0.2 select_reduce_fusion
  82.7 0.6 copy-done.3
  83.3 0.5 fusion.28
  83.8 0.4 fusion.9
  84.2 0.3 fusion.1
  84.5 0.9 fusion.8
  85.4 0.3 convolution_multiply_fusion
  86.1 1.3 collective-permute-start.10
  87.4 4.7 %collective-permute-start.9 = (bf16[2,2,64,128]{3,2,1,0:T(8,128)(2,1)S(1)}, bf16[2,2,64,128]{3,2,1,0:T(8,128)(2,1)S(1)}, u32[]{:S(2)}, u32[]{:S(2)}) collective-permute-start(bf16[2,2,64,128]{3,2,1,0:T(8,128)(2,1)S(1)} %get-tuple-element.50), channel_id=1, source_target_pairs={{0,4},{4,8},{8,12},{12,16},{16,20},{20,24},{24,28},{1,5},{5,9},{9,... | collective-permute-start | bytes 196616 | tf_op jit(solution)/shard_map/ppermute | solution.py:15
  92.2 0.9 copy.63
  93.1 1.9 %fusion.2 = bf16[3,2,2,2,64,128]{5,3,4,1,2,0:T(2,128)(2,1)S(1)} fusion(f32[2,2,2,3,64,128]{5,4,3,2,1,0:T(8,128)S(1)} %pad_maximum_fusion, s32[2,2,3]{1,0,2:T(2,128)S(1)} %copy.53), kind=kOutput, calls=%fused_computation.8 | convolution fusion | flops 4915224 | bytes 1179696 | tf_op jit(solution)/shard_map/hqjl,chqjbd->jchlbd/dot_general | solution.py:151
  95.0 0.3 fusion.50
  95.5 2.1 %collective-permute-start.14 = (bf16[2,2,128,128]{3,2,1,0:T(8,128)(2,1)S(1)}, bf16[2,2,128,128]{3,2,1,0:T(8,128)(2,1)S(1)}, u32[]{:S(2)}, u32[]{:S(2)}) collective-permute-start(bf16[2,2,128,128]{3,2,1,0:T(8,128)(2,1)S(1)} %bitcast.125), channel_id=1, source_target_pairs={{0,4},{4,0},{8,12},{12,8},{16,20},{20,16},{24,28},{28,24},{1,5},{5... | collective-permute-start | bytes 393224 | tf_op jit(solution)/shard_map/ppermute | solution.py:24
  98.1 2.6 %scatter-add.9 = f32[2,2,2,64,128]{4,2,3,1,0:T(2,128)S(1)} dynamic-update-slice(f32[2,2,2,64,128]{4,2,3,1,0:T(2,128)S(1)} %copy.62, f32[2,2,1,64,128]{4,2,3,1,0:T(1,128)S(1)} %add.68, s32[]{:T(128)} %constant.122.clone.1, s32[]{:T(128)} %constant.122.clone.1, s32[]{:T(128)} %constant.126.clone.1, s32[]{:T(128)} %constant.122.clone.1, s32[]{:T(128)} %constant.122.clone.1) | dynamic-update-slice | bytes 262148 | tf_op jit(solution)/shard_map/scatter-add | solution.py:138
  100.9 0.9 collective-permute-done.14
  101.9 1.2 collective-permute-start.15
  103.3 0.8 collective-permute-start.12
  104.2 4.2 %collective-permute-done.18 = bf16[2,2,128,128]{3,2,1,0:T(8,128)(2,1)S(1)} collective-permute-done((bf16[2,2,128,128]{3,2,1,0:T(8,128)(2,1)S(1)}, bf16[2,2,128,128]{3,2,1,0:T(8,128)(2,1)S(1)}, u32[]{:S(2)}, u32[]{:S(2)}) %collective-permute-start.18) | collective-permute-done | bytes 131104 | tf_op jit(solution)/shard_map/ppermute | solution.py:24
  108.5 1.4 collective-permute-done.15
  110.0 1.5 collective-permute-start.16
  111.7 1.5 collective-permute-start.13
  113.2 4.5 %collective-permute-done.19 = bf16[2,2,128,128]{3,2,1,0:T(8,128)(2,1)S(1)} collective-permute-done((bf16[2,2,128,128]{3,2,1,0:T(8,128)(2,1)S(1)}, bf16[2,2,128,128]{3,2,1,0:T(8,128)(2,1)S(1)}, u32[]{:S(2)}, u32[]{:S(2)}) %collective-permute-start.19) | collective-permute-done | bytes 131104 | tf_op jit(solution)/shard_map/ppermute | solution.py:24
  117.7 1.6 collective-permute-done.16
  119.4 1.4 collective-permute-done.13
  121.0 43.2 %all-reduce.6.cloned.1.call-done = f32[2,2,2,64,128]{4,2,3,1,0:T(2,128)} async-done(((f32[2,2,2,64,128]{4,2,3,1,0:T(2,128)}), f32[2,2,2,64,128]{4,2,3,1,0:T(2,128)}) %all-reduce.6.cloned.1.call-update) | async-done | bytes 262160 | tf_op jit(solution)/shard_map/psum | solution.py:142
  164.1 1.8 %fusion.7 = bf16[2,2,2,64,128]{4,2,3,1,0:T(2,128)(2,1)S(1)} fusion(f32[2,2,2,64,128]{4,2,3,1,0:T(2,128)S(1)} %scatter-add.9, f32[2,2,2,64,128]{4,2,3,1,0:T(2,128)} %all-reduce.6.cloned.1.call-done, f32[2,2,2,64,128]{4,3,2,1,0:T(8,128)S(1)} %bitcast.136, pred[2]{0:T(512)(128)(4,1)S(1)} %get-tuple-element.63, s32[2]{0:T(128)S(1)} %get-tuple-element.39), kind=kOutput, calls=%fused_computation.14 | convolution fusion | flops 1769480 | bytes 917514 | tf_op jit(solution)/shard_map/gn,chgbd->chnbd/dot_general | solution.py:146
  166.0 0.6 copy.69
  166.7 0.6 copy.70
  (90 shorter events, 4.9 us)
Async XLA Ops:
  7.2 74.9 %copy-start = (bf16[2,128,128]{2,1,0:T(8,128)(2,1)S(1)}, bf16[2,128,128]{2,1,0:T(8,128)(2,1)}, u32[]{:S(2)}) copy-start(bf16[2,128,128]{2,1,0:T(8,128)(2,1)} %param.10) | copy-start | bytes 196612
  7.2 157.0 %all-reduce.6.cloned.1.call-start = ((), (), s32[]{:S(2)}) async-start(), calls=%async_computation | async-start | bytes 524288 | tf_op jit(solution)/shard_map/psum | solution.py:142
  7.2 7.7 %copy-start.1 = (bf16[2,128,128]{2,1,0:T(8,128)(2,1)S(1)}, bf16[2,128,128]{2,1,0:T(8,128)(2,1)}, u32[]{:S(2)}) copy-start(bf16[2,128,128]{2,1,0:T(8,128)(2,1)} %param.11) | copy-start | bytes 196612
  7.2 7.7 %copy-start.2 = (bf16[2,128,128]{2,1,0:T(8,128)(2,1)S(1)}, bf16[2,128,128]{2,1,0:T(8,128)(2,1)}, u32[]{:S(2)}) copy-start(bf16[2,128,128]{2,1,0:T(8,128)(2,1)} %param.12) | copy-start | bytes 196612
  8.1 51.4 %collective-permute-start.1 = (bf16[2,2,64,128]{3,2,1,0:T(8,128)(2,1)S(1)}, bf16[2,2,64,128]{3,2,1,0:T(8,128)(2,1)S(1)}, u32[]{:S(2)}, u32[]{:S(2)}) collective-permute-start(bf16[2,2,64,128]{3,2,1,0:T(8,128)(2,1)S(1)} %get-tuple-element.61), channel_id=1, source_target_pairs={{4,0},{8,4},{12,8},{16,12},{20,16},{24,20},{28,24},{5,1},{9,5},{13... | collective-permute-start | bytes 196616 | tf_op jit(solution)/shard_map/ppermute | solution.py:16
  9.4 50.1 %collective-permute-start = (bf16[2,2,64,128]{3,2,1,0:T(8,128)(2,1)S(1)}, bf16[2,2,64,128]{3,2,1,0:T(8,128)(2,1)S(1)}, u32[]{:S(2)}, u32[]{:S(2)}) collective-permute-start(bf16[2,2,64,128]{3,2,1,0:T(8,128)(2,1)S(1)} %get-tuple-element.60), channel_id=1, source_target_pairs={{0,4},{4,8},{8,12},{12,16},{16,20},{20,24},{24,28},{1,5},{5,9},{9,... | collective-permute-start | bytes 196616 | tf_op jit(solution)/shard_map/ppermute | solution.py:15
  15.0 3.0 %copy-start.4 = (s32[2,2,3]{2,1,0:T(2,128)S(1)}, s32[2,2,3]{2,1,0:T(2,128)}, u32[]{:S(2)}) copy-start(s32[2,2,3]{2,1,0:T(2,128)} %param.14) | copy-start | bytes 148
  15.0 45.0 %collective-permute-start.2 = (bf16[2,2,128,128]{3,2,1,0:T(8,128)(2,1)S(1)}, bf16[2,2,128,128]{3,2,1,0:T(8,128)(2,1)S(1)}, u32[]{:S(2)}, u32[]{:S(2)}) collective-permute-start(bf16[2,2,128,128]{3,2,1,0:T(8,128)(2,1)S(1)} %pad_maximum_fusion.7), channel_id=1, source_target_pairs={{0,4},{4,0},{8,12},{12,8},{16,20},{20,16},{24,28},{28,24},{1,5},{5... | collective-permute-start | bytes 393224 | tf_op jit(solution)/shard_map/ppermute | solution.py:24
  18.0 0.7 copy-start.5
  58.0 0.7 slice-start
  60.2 6.4 %collective-permute-start.7 = (bf16[2,2,128,128]{3,2,1,0:T(8,128)(2,1)S(1)}, bf16[2,2,128,128]{3,2,1,0:T(8,128)(2,1)S(1)}, u32[]{:S(2)}, u32[]{:S(2)}) collective-permute-start(bf16[2,2,128,128]{3,2,1,0:T(8,128)(2,1)S(1)} %get-tuple-element.53), channel_id=1, source_target_pairs={{0,8},{4,12},{8,0},{12,4},{16,24},{20,28},{24,16},{28,20},{1,9},{5... | collective-permute-start | bytes 393224 | tf_op jit(solution)/shard_map/ppermute | solution.py:24
  60.4 9.2 %collective-permute-start.5 = (bf16[2,2,128,128]{3,2,1,0:T(8,128)(2,1)S(1)}, bf16[2,2,128,128]{3,2,1,0:T(8,128)(2,1)S(1)}, u32[]{:S(2)}, u32[]{:S(2)}) collective-permute-start(bf16[2,2,128,128]{3,2,1,0:T(8,128)(2,1)S(1)} %get-tuple-element.54), channel_id=1, source_target_pairs={{0,8},{4,12},{8,0},{12,4},{16,24},{20,28},{24,16},{28,20},{1,9},{5... | collective-permute-start | bytes 393224 | tf_op jit(solution)/shard_map/ppermute | solution.py:24
  62.5 8.6 %collective-permute-start.3 = (bf16[2,2,128,128]{3,2,1,0:T(8,128)(2,1)S(1)}, bf16[2,2,128,128]{3,2,1,0:T(8,128)(2,1)S(1)}, u32[]{:S(2)}, u32[]{:S(2)}) collective-permute-start(bf16[2,2,128,128]{3,2,1,0:T(8,128)(2,1)S(1)} %get-tuple-element.52), channel_id=1, source_target_pairs={{0,8},{4,12},{8,0},{12,4},{16,24},{20,28},{24,16},{28,20},{1,9},{5... | collective-permute-start | bytes 393224 | tf_op jit(solution)/shard_map/ppermute | solution.py:24
  66.7 9.6 %collective-permute-start.8 = (bf16[2,2,128,128]{3,2,1,0:T(8,128)(2,1)S(1)}, bf16[2,2,128,128]{3,2,1,0:T(8,128)(2,1)S(1)}, u32[]{:S(2)}, u32[]{:S(2)}) collective-permute-start(bf16[2,2,128,128]{3,2,1,0:T(8,128)(2,1)S(1)} %broadcast_select_fusion.3), channel_id=1, source_target_pairs={{0,16},{4,20},{8,24},{12,28},{16,0},{20,4},{24,8},{28,12},{1,17},{... | collective-permute-start | bytes 393224 | tf_op jit(solution)/shard_map/ppermute | solution.py:24
  69.7 8.4 %collective-permute-start.6 = (bf16[2,2,128,128]{3,2,1,0:T(8,128)(2,1)S(1)}, bf16[2,2,128,128]{3,2,1,0:T(8,128)(2,1)S(1)}, u32[]{:S(2)}, u32[]{:S(2)}) collective-permute-start(bf16[2,2,128,128]{3,2,1,0:T(8,128)(2,1)S(1)} %broadcast_select_fusion.8), channel_id=1, source_target_pairs={{0,16},{4,20},{8,24},{12,28},{16,0},{20,4},{24,8},{28,12},{1,17},{... | collective-permute-start | bytes 393224 | tf_op jit(solution)/shard_map/ppermute | solution.py:24
  71.2 8.6 %collective-permute-start.4 = (bf16[2,2,128,128]{3,2,1,0:T(8,128)(2,1)S(1)}, bf16[2,2,128,128]{3,2,1,0:T(8,128)(2,1)S(1)}, u32[]{:S(2)}, u32[]{:S(2)}) collective-permute-start(bf16[2,2,128,128]{3,2,1,0:T(8,128)(2,1)S(1)} %broadcast_select_fusion.13), channel_id=1, source_target_pairs={{0,16},{4,20},{8,24},{12,28},{16,0},{20,4},{24,8},{28,12},{1,17},{... | collective-permute-start | bytes 393224 | tf_op jit(solution)/shard_map/ppermute | solution.py:24
  82.4 0.8 copy-start.3
  86.1 11.6 %collective-permute-start.10 = (bf16[2,2,64,128]{3,2,1,0:T(8,128)(2,1)S(1)}, bf16[2,2,64,128]{3,2,1,0:T(8,128)(2,1)S(1)}, u32[]{:S(2)}, u32[]{:S(2)}) collective-permute-start(bf16[2,2,64,128]{3,2,1,0:T(8,128)(2,1)S(1)} %get-tuple-element.51), channel_id=1, source_target_pairs={{4,0},{8,4},{12,8},{16,12},{20,16},{24,20},{28,24},{5,1},{9,5},{13... | collective-permute-start | bytes 196616 | tf_op jit(solution)/shard_map/ppermute | solution.py:16
  87.4 10.3 %collective-permute-start.9 = (bf16[2,2,64,128]{3,2,1,0:T(8,128)(2,1)S(1)}, bf16[2,2,64,128]{3,2,1,0:T(8,128)(2,1)S(1)}, u32[]{:S(2)}, u32[]{:S(2)}) collective-permute-start(bf16[2,2,64,128]{3,2,1,0:T(8,128)(2,1)S(1)} %get-tuple-element.50), channel_id=1, source_target_pairs={{0,4},{4,8},{8,12},{12,16},{16,20},{20,24},{24,28},{1,5},{5,9},{9,... | collective-permute-start | bytes 196616 | tf_op jit(solution)/shard_map/ppermute | solution.py:15
  95.4 5.4 %collective-permute-start.17 = (bf16[2,2,128,128]{3,2,1,0:T(8,128)(2,1)S(1)}, bf16[2,2,128,128]{3,2,1,0:T(8,128)(2,1)S(1)}, u32[]{:S(2)}, u32[]{:S(2)}) collective-permute-start(bf16[2,2,128,128]{3,2,1,0:T(8,128)(2,1)S(1)} %bitcast.127), channel_id=1, source_target_pairs={{0,4},{4,0},{8,12},{12,8},{16,20},{20,16},{24,28},{28,24},{1,5},{5... | collective-permute-start | bytes 393224 | tf_op jit(solution)/shard_map/ppermute | solution.py:24
  95.5 6.3 %collective-permute-start.14 = (bf16[2,2,128,128]{3,2,1,0:T(8,128)(2,1)S(1)}, bf16[2,2,128,128]{3,2,1,0:T(8,128)(2,1)S(1)}, u32[]{:S(2)}, u32[]{:S(2)}) collective-permute-start(bf16[2,2,128,128]{3,2,1,0:T(8,128)(2,1)S(1)} %bitcast.125), channel_id=1, source_target_pairs={{0,4},{4,0},{8,12},{12,8},{16,20},{20,16},{24,28},{28,24},{1,5},{5... | collective-permute-start | bytes 393224 | tf_op jit(solution)/shard_map/ppermute | solution.py:24
  97.6 5.6 %collective-permute-start.11 = (bf16[2,2,128,128]{3,2,1,0:T(8,128)(2,1)S(1)}, bf16[2,2,128,128]{3,2,1,0:T(8,128)(2,1)S(1)}, u32[]{:S(2)}, u32[]{:S(2)}) collective-permute-start(bf16[2,2,128,128]{3,2,1,0:T(8,128)(2,1)S(1)} %bitcast.123), channel_id=1, source_target_pairs={{0,4},{4,0},{8,12},{12,8},{16,20},{20,16},{24,28},{28,24},{1,5},{5... | collective-permute-start | bytes 393224 | tf_op jit(solution)/shard_map/ppermute | solution.py:24
  100.9 7.5 %collective-permute-start.18 = (bf16[2,2,128,128]{3,2,1,0:T(8,128)(2,1)S(1)}, bf16[2,2,128,128]{3,2,1,0:T(8,128)(2,1)S(1)}, u32[]{:S(2)}, u32[]{:S(2)}) collective-permute-start(bf16[2,2,128,128]{3,2,1,0:T(8,128)(2,1)S(1)} %broadcast_select_fusion), channel_id=1, source_target_pairs={{0,8},{4,12},{8,0},{12,4},{16,24},{20,28},{24,16},{28,20},{1,9},{5... | collective-permute-start | bytes 393224 | tf_op jit(solution)/shard_map/ppermute | solution.py:24
  101.9 8.0 %collective-permute-start.15 = (bf16[2,2,128,128]{3,2,1,0:T(8,128)(2,1)S(1)}, bf16[2,2,128,128]{3,2,1,0:T(8,128)(2,1)S(1)}, u32[]{:S(2)}, u32[]{:S(2)}) collective-permute-start(bf16[2,2,128,128]{3,2,1,0:T(8,128)(2,1)S(1)} %broadcast_select_fusion.5), channel_id=1, source_target_pairs={{0,8},{4,12},{8,0},{12,4},{16,24},{20,28},{24,16},{28,20},{1,9},{5... | collective-permute-start | bytes 393224 | tf_op jit(solution)/shard_map/ppermute | solution.py:24
  103.3 8.2 %collective-permute-start.12 = (bf16[2,2,128,128]{3,2,1,0:T(8,128)(2,1)S(1)}, bf16[2,2,128,128]{3,2,1,0:T(8,128)(2,1)S(1)}, u32[]{:S(2)}, u32[]{:S(2)}) collective-permute-start(bf16[2,2,128,128]{3,2,1,0:T(8,128)(2,1)S(1)} %broadcast_select_fusion.10), channel_id=1, source_target_pairs={{0,8},{4,12},{8,0},{12,4},{16,24},{20,28},{24,16},{28,20},{1,9},{5... | collective-permute-start | bytes 393224 | tf_op jit(solution)/shard_map/ppermute | solution.py:24
  108.4 9.2 %collective-permute-start.19 = (bf16[2,2,128,128]{3,2,1,0:T(8,128)(2,1)S(1)}, bf16[2,2,128,128]{3,2,1,0:T(8,128)(2,1)S(1)}, u32[]{:S(2)}, u32[]{:S(2)}) collective-permute-start(bf16[2,2,128,128]{3,2,1,0:T(8,128)(2,1)S(1)} %broadcast_select_fusion.2), channel_id=1, source_target_pairs={{0,16},{4,20},{8,24},{12,28},{16,0},{20,4},{24,8},{28,12},{1,17},{... | collective-permute-start | bytes 393224 | tf_op jit(solution)/shard_map/ppermute | solution.py:24
  110.0 9.3 %collective-permute-start.16 = (bf16[2,2,128,128]{3,2,1,0:T(8,128)(2,1)S(1)}, bf16[2,2,128,128]{3,2,1,0:T(8,128)(2,1)S(1)}, u32[]{:S(2)}, u32[]{:S(2)}) collective-permute-start(bf16[2,2,128,128]{3,2,1,0:T(8,128)(2,1)S(1)} %broadcast_select_fusion.7), channel_id=1, source_target_pairs={{0,16},{4,20},{8,24},{12,28},{16,0},{20,4},{24,8},{28,12},{1,17},{... | collective-permute-start | bytes 393224 | tf_op jit(solution)/shard_map/ppermute | solution.py:24
  111.7 9.1 %collective-permute-start.13 = (bf16[2,2,128,128]{3,2,1,0:T(8,128)(2,1)S(1)}, bf16[2,2,128,128]{3,2,1,0:T(8,128)(2,1)S(1)}, u32[]{:S(2)}, u32[]{:S(2)}) collective-permute-start(bf16[2,2,128,128]{3,2,1,0:T(8,128)(2,1)S(1)} %broadcast_select_fusion.12), channel_id=1, source_target_pairs={{0,16},{4,20},{8,24},{12,28},{16,0},{20,4},{24,8},{28,12},{1,17},{... | collective-permute-start | bytes 393224 | tf_op jit(solution)/shard_map/ppermute | solution.py:24
Sparse Core Ops, SparseCore 0:
  93.2 70.8 all-reduce.5
where the time goes:
time: 175 us; the launch traced here: 174 us
  waiting for transfers between devices  71.9 us (41%)
  blocking collectives  38.6 us (22%)
  starting transfers between devices  27.4 us (16%)
  between operations  14.6 us (8%)
  local copies, waits for them, and re-layouts  10.8 us (6%)
  matrix products  7.31 us (4%)
  other arithmetic  3.48 us (2%)
    psum x1, waiting for transfers between devices, on_device(): global_total = lax.psum(global_part, 'seq')  43.2 us
    psum x1, blocking collectives, on_device(): global_sum = lax.psum(picked * owned[None, None, :, None, None], 'seq')  38.6 us
    ppermute x16, waiting for transfers between devices, swapped(): return lax.ppermute(value, axis, pairs)  28.7 us
    ppermute x16, starting transfers between devices, swapped(): return lax.ppermute(value, axis, pairs)  14.5 us
    ppermute x2, starting transfers between devices, with_halo(): before = lax.ppermute(last, axis, up)  10.3 us
  transfers between devices with their start and end apart: 21, of which 14 were waited for; matrix products, arithmetic and copies ran while one was open for 6% of the time, Pallas kernels for 0%

commit v1 on v0

--- a/solution.py
+++ b/solution.py
@@ -1,8 +1,17 @@
+import functools
 import math
 import jax
 import jax.numpy as jnp
 from jax import lax
 from jax.sharding import PartitionSpec as P
+
+
+def produce_tokens(view, shard_axis):
+    left_arr = jax.lax.all_gather(view, shard_axis)
+    return jnp.sum(left_arr, axis=0)
+
+
+mix_ports_now = functools.partial(produce_tokens, shard_axis="seq")
 
 
 def with_halo(value, sides, width):
@@ -139,7 +148,7 @@
         rim_back[:, :, 3 * block_rows : 4 * block_rows]
     )
     global_part = jnp.sum(grads[:, :, :, 3 : 3 + global_count], axis=2)
-    global_total = lax.psum(global_part, "seq")
+    global_total = mix_ports_now(global_part)
     global_onehot = (
         (global_local[:, None] == block_range[None, :]) & (global_owner == device)[:, None]
     ).astype(jnp.float32)

time: 175 us -> 154 us (0.88)
  waiting for transfers between devices: 71.9 us -> 50.1 us
  other arithmetic: 3.48 us -> 9.88 us
  starting transfers between devices: 27.4 us -> 24.9 us
  local copies, waits for them, and re-layouts: 10.8 us -> 8.73 us
    psum x1 -> x0, waiting for transfers between devices: 43.2 us -> none  [on_device(): global_total = lax.psum(global_part, 'seq')]
    ppermute x16, waiting for transfers between devices: 28.7 us -> 45.1 us  [swapped(): return lax.ppermute(value, axis, pairs)]
    all_gather x0 -> x1, waiting for transfers between devices: none -> 4.92 us  [produce_tokens(): left_arr = jax.lax.all_gather(view, shard_axis)]
    ppermute x16, starting transfers between devices: 14.5 us -> 11.9 us  [swapped(): return lax.ppermute(value, axis, pairs)]
  transfers between devices with their start and end apart: 21 -> 21, of which waited for: 14 -> 14; matrix products, arithmetic and copies ran while one was open for 6% -> 10% of each run, Pallas kernels for 0% -> 0%
where the time goes in v1:
time: 154 us; the launch traced here: 153 us
  waiting for transfers between devices  50.1 us (33%)
  blocking collectives  38.6 us (25%)
  starting transfers between devices  24.9 us (16%)
  between operations  14.6 us (9%)
  other arithmetic  9.88 us (6%)
  local copies, waits for them, and re-layouts  8.73 us (6%)
  matrix products  6.42 us (4%)
    ppermute x16, waiting for transfers between devices, swapped(): return lax.ppermute(value, axis, pairs)  45.1 us
    psum x1, blocking collectives, on_device(): global_sum = lax.psum(picked * owned[None, None, :, None, None], 'seq')  38.6 us
    ppermute x16, starting transfers between devices, swapped(): return lax.ppermute(value, axis, pairs)  11.9 us
    ppermute x2, starting transfers between devices, with_halo(): before = lax.ppermute(last, axis, up)  10.3 us
    all_gather x1, waiting for transfers between devices, produce_tokens(): left_arr = jax.lax.all_gather(view, shard_axis)  4.92 us
  transfers between devices with their start and end apart: 21, of which 14 were waited for; matrix products, arithmetic and copies ran while one was open for 10% of the time, Pallas kernels for 0%

profile of v1, /device:TPU:0, one launch (start us, length us, event | category | flops | bytes accessed | tf_op | source)
XLA Modules:
  0.0 153.2 jit_solution(9887296763784880503)
XLA Ops:
  7.2 0.9 fusion.25
  8.1 1.3 collective-permute-start.1
  9.4 5.5 %collective-permute-start = (bf16[2,2,64,128]{3,2,1,0:T(8,128)(2,1)S(1)}, bf16[2,2,64,128]{3,2,1,0:T(8,128)(2,1)S(1)}, u32[]{:S(2)}, u32[]{:S(2)}) collective-permute-start(bf16[2,2,64,128]{3,2,1,0:T(8,128)(2,1)S(1)} %get-tuple-element.60), channel_id=1, source_target_pairs={{0,4},{4,8},{8,12},{12,16},{16,20},{20,24},{24,28},{1,5},{5,9},{9,... | collective-permute-start | bytes 196616 | tf_op jit(solution)/shard_map/ppermute | solution.py:24
  14.9 0.9 pad_maximum_fusion.7
  15.8 3.0 %collective-permute-start.2 = (bf16[2,2,128,128]{3,2,1,0:T(8,128)(2,1)S(1)}, bf16[2,2,128,128]{3,2,1,0:T(8,128)(2,1)S(1)}, u32[]{:S(2)}, u32[]{:S(2)}) collective-permute-start(bf16[2,2,128,128]{3,2,1,0:T(8,128)(2,1)S(1)} %pad_maximum_fusion.7), channel_id=1, source_target_pairs={{0,4},{4,0},{8,12},{12,8},{16,20},{20,16},{24,28},{28,24},{1,5},{5... | collective-permute-start | bytes 393224 | tf_op jit(solution)/shard_map/ppermute | solution.py:33
  18.8 0.7 slice.172
  19.5 0.7 and_select_fusion
  20.2 0.7 compare_and_fusion
  20.9 0.9 pad_maximum_fusion.8
  21.8 0.6 gather_fusion
  22.5 38.6 %all-reduce.4 = bf16[2,2,2,64,128]{4,3,1,0,2:T(8,128)(2,1)S(1)} all-reduce(f32[2,2,2,64,128]{4,3,1,0,2:T(8,128)S(1)} %multiply_bitcast_fusion), channel_id=1, replica_groups=mesh['seq'=8,'head'=4] {'seq'}, use_global_device_ids=true, to_apply=%region_0.1 | all-reduce | flops 65536 | bytes 393216 | tf_op jit(solution)/shard_map/psum | solution.py:67
  61.9 0.9 pad_maximum_fusion.6
  63.7 2.1 %collective-permute-start.5 = (bf16[2,2,128,128]{3,2,1,0:T(8,128)(2,1)S(1)}, bf16[2,2,128,128]{3,2,1,0:T(8,128)(2,1)S(1)}, u32[]{:S(2)}, u32[]{:S(2)}) collective-permute-start(bf16[2,2,128,128]{3,2,1,0:T(8,128)(2,1)S(1)} %get-tuple-element.54), channel_id=1, source_target_pairs={{0,8},{4,12},{8,0},{12,4},{16,24},{20,28},{24,16},{28,20},{1,9},{5... | collective-permute-start | bytes 393224 | tf_op jit(solution)/shard_map/ppermute | solution.py:33
  65.9 4.0 %collective-permute-done.7 = bf16[2,2,128,128]{3,2,1,0:T(8,128)(2,1)S(1)} collective-permute-done((bf16[2,2,128,128]{3,2,1,0:T(8,128)(2,1)S(1)}, bf16[2,2,128,128]{3,2,1,0:T(8,128)(2,1)S(1)}, u32[]{:S(2)}, u32[]{:S(2)}) %collective-permute-start.7) | collective-permute-done | bytes 131104 | tf_op jit(solution)/shard_map/ppermute | solution.py:33
  70.0 2.9 %collective-permute-done.5 = bf16[2,2,128,128]{3,2,1,0:T(8,128)(2,1)S(1)} collective-permute-done((bf16[2,2,128,128]{3,2,1,0:T(8,128)(2,1)S(1)}, bf16[2,2,128,128]{3,2,1,0:T(8,128)(2,1)S(1)}, u32[]{:S(2)}, u32[]{:S(2)}) %collective-permute-start.5) | collective-permute-done | bytes 131104 | tf_op jit(solution)/shard_map/ppermute | solution.py:33
  73.1 1.2 collective-permute-done.3
  74.4 1.7 %collective-permute-start.4 = (bf16[2,2,128,128]{3,2,1,0:T(8,128)(2,1)S(1)}, bf16[2,2,128,128]{3,2,1,0:T(8,128)(2,1)S(1)}, u32[]{:S(2)}, u32[]{:S(2)}) collective-permute-start(bf16[2,2,128,128]{3,2,1,0:T(8,128)(2,1)S(1)} %broadcast_select_fusion.13), channel_id=1, source_target_pairs={{0,16},{4,20},{8,24},{12,28},{16,0},{20,4},{24,8},{28,12},{1,17},{... | collective-permute-start | bytes 393224 | tf_op jit(solution)/shard_map/ppermute | solution.py:33
  76.2 3.5 %collective-permute-done.8 = bf16[2,2,128,128]{3,2,1,0:T(8,128)(2,1)S(1)} collective-permute-done((bf16[2,2,128,128]{3,2,1,0:T(8,128)(2,1)S(1)}, bf16[2,2,128,128]{3,2,1,0:T(8,128)(2,1)S(1)}, u32[]{:S(2)}, u32[]{:S(2)}) %collective-permute-start.8) | collective-permute-done | bytes 131104 | tf_op jit(solution)/shard_map/ppermute | solution.py:33
  79.9 1.8 %collective-permute-done.6 = bf16[2,2,128,128]{3,2,1,0:T(8,128)(2,1)S(1)} collective-permute-done((bf16[2,2,128,128]{3,2,1,0:T(8,128)(2,1)S(1)}, bf16[2,2,128,128]{3,2,1,0:T(8,128)(2,1)S(1)}, u32[]{:S(2)}, u32[]{:S(2)}) %collective-permute-start.6) | collective-permute-done | bytes 131104 | tf_op jit(solution)/shard_map/ppermute | solution.py:33
  81.9 1.2 collective-permute-done.4
  83.3 0.8 fusion.4
  84.1 1.2 fusion.50
  85.3 0.4 select_reduce_fusion.1
  86.0 0.5 fusion.29
  86.5 0.4 fusion.9
  87.2 0.4 convolution_multiply_fusion
  87.7 0.7 maximum_reduce_fusion
  88.6 1.4 collective-permute-start.10
  90.1 4.7 %collective-permute-start.9 = (bf16[2,2,64,128]{3,2,1,0:T(8,128)(2,1)S(1)}, bf16[2,2,64,128]{3,2,1,0:T(8,128)(2,1)S(1)}, u32[]{:S(2)}, u32[]{:S(2)}) collective-permute-start(bf16[2,2,64,128]{3,2,1,0:T(8,128)(2,1)S(1)} %get-tuple-element.50), channel_id=1, source_target_pairs={{0,4},{4,8},{8,12},{12,16},{16,20},{20,24},{24,28},{1,5},{5,9},{9,... | collective-permute-start | bytes 196616 | tf_op jit(solution)/shard_map/ppermute | solution.py:24
  94.9 0.9 fusion.8
  95.7 1.9 %fusion.2 = bf16[3,2,2,2,64,128]{5,3,4,1,2,0:T(2,128)(2,1)S(1)} fusion(f32[2,2,2,3,64,128]{5,4,3,2,1,0:T(8,128)S(1)} %pad_maximum_fusion, s32[2,2,3]{1,0,2:T(2,128)S(1)} %copy.78), kind=kOutput, calls=%fused_computation.8 | convolution fusion | flops 4915224 | bytes 1179696 | tf_op jit(solution)/shard_map/hqjl,chqjbd->jchlbd/dot_general | solution.py:160
  97.7 0.3 fusion.51
  98.2 2.1 %collective-permute-start.14 = (bf16[2,2,128,128]{3,2,1,0:T(8,128)(2,1)S(1)}, bf16[2,2,128,128]{3,2,1,0:T(8,128)(2,1)S(1)}, u32[]{:S(2)}, u32[]{:S(2)}) collective-permute-start(bf16[2,2,128,128]{3,2,1,0:T(8,128)(2,1)S(1)} %bitcast.126), channel_id=1, source_target_pairs={{0,4},{4,0},{8,12},{12,8},{16,20},{20,16},{24,28},{28,24},{1,5},{5... | collective-permute-start | bytes 393224 | tf_op jit(solution)/shard_map/ppermute | solution.py:33
  100.8 2.6 %scatter-add.9 = f32[2,2,2,64,128]{4,2,3,1,0:T(2,128)S(1)} dynamic-update-slice(f32[2,2,2,64,128]{4,2,3,1,0:T(2,128)S(1)} %copy.87, f32[2,2,1,64,128]{4,2,3,1,0:T(1,128)S(1)} %add.66, s32[]{:T(128)} %constant.122.clone.1, s32[]{:T(128)} %constant.122.clone.1, s32[]{:T(128)} %constant.126.clone.1, s32[]{:T(128)} %constant.122.clone.1, s32[]{:T(128)} %constant.122.clone.1) | dynamic-update-slice | bytes 262148 | tf_op jit(solution)/shard_map/scatter-add | solution.py:147
  103.6 0.9 collective-permute-done.14
  104.6 1.2 collective-permute-start.15
  106.0 0.8 collective-permute-start.12
  106.8 5.3 %collective-permute-done.18 = bf16[2,2,128,128]{3,2,1,0:T(8,128)(2,1)S(1)} collective-permute-done((bf16[2,2,128,128]{3,2,1,0:T(8,128)(2,1)S(1)}, bf16[2,2,128,128]{3,2,1,0:T(8,128)(2,1)S(1)}, u32[]{:S(2)}, u32[]{:S(2)}) %collective-permute-start.18) | collective-permute-done | bytes 131104 | tf_op jit(solution)/shard_map/ppermute | solution.py:33
  112.3 3.5 %collective-permute-done.15 = bf16[2,2,128,128]{3,2,1,0:T(8,128)(2,1)S(1)} collective-permute-done((bf16[2,2,128,128]{3,2,1,0:T(8,128)(2,1)S(1)}, bf16[2,2,128,128]{3,2,1,0:T(8,128)(2,1)S(1)}, u32[]{:S(2)}, u32[]{:S(2)}) %collective-permute-start.15) | collective-permute-done | bytes 131104 | tf_op jit(solution)/shard_map/ppermute | solution.py:33
  116.0 2.6 %collective-permute-done.12 = bf16[2,2,128,128]{3,2,1,0:T(8,128)(2,1)S(1)} collective-permute-done((bf16[2,2,128,128]{3,2,1,0:T(8,128)(2,1)S(1)}, bf16[2,2,128,128]{3,2,1,0:T(8,128)(2,1)S(1)}, u32[]{:S(2)}, u32[]{:S(2)}) %collective-permute-start.12) | collective-permute-done | bytes 131104 | tf_op jit(solution)/shard_map/ppermute | solution.py:33
  118.7 0.3 collective-permute-start.13
  119.1 11.3 %collective-permute-done.16 = bf16[2,2,128,128]{3,2,1,0:T(8,128)(2,1)S(1)} collective-permute-done((bf16[2,2,128,128]{3,2,1,0:T(8,128)(2,1)S(1)}, bf16[2,2,128,128]{3,2,1,0:T(8,128)(2,1)S(1)}, u32[]{:S(2)}, u32[]{:S(2)}) %collective-permute-start.16) | collective-permute-done | bytes 131104 | tf_op jit(solution)/shard_map/ppermute | solution.py:33
  130.5 6.8 %collective-permute-done.13 = bf16[2,2,128,128]{3,2,1,0:T(8,128)(2,1)S(1)} collective-permute-done((bf16[2,2,128,128]{3,2,1,0:T(8,128)(2,1)S(1)}, bf16[2,2,128,128]{3,2,1,0:T(8,128)(2,1)S(1)}, u32[]{:S(2)}, u32[]{:S(2)}) %collective-permute-start.13) | collective-permute-done | bytes 131104 | tf_op jit(solution)/shard_map/ppermute | solution.py:33
  137.4 4.9 %all-gather.3.cloned.1.call-done = f32[16,2,2,64,128]{4,3,2,1,0:T(8,128)} async-done(((f32[2,2,2,64,128]{4,3,2,1,0:T(8,128)}), f32[16,2,2,64,128]{4,3,2,1,0:T(8,128)}) %all-gather.3.cloned.1.call-update) | async-done | bytes 2097168 | tf_op jit(solution)/shard_map/all_gather | solution.py:10
  142.4 1.7 %reduce_sum.48 = f32[2,2,2,64,128]{4,3,2,1,0:T(8,128)S(1)} reduce(f32[8,2,2,2,64,128]{5,4,3,2,1,0:T(8,128)} %bitcast.107, f32[]{:T(128)} %constant.134.clone.1), dimensions={0}, to_apply=%region_5.6 | reduce | flops 458752 | bytes 2359300 | tf_op jit(solution)/shard_map/reduce_sum | solution.py:11
  144.1 0.9 fusion.7
  145.1 0.6 copy.95
  145.7 0.6 copy.96
  (89 shorter events, 5.7 us)
Async XLA Ops:
  7.2 78.1 %copy-start = (bf16[2,128,128]{2,1,0:T(8,128)(2,1)S(1)}, bf16[2,128,128]{2,1,0:T(8,128)(2,1)}, u32[]{:S(2)}) copy-start(bf16[2,128,128]{2,1,0:T(8,128)(2,1)} %param.10) | copy-start | bytes 196612
  7.2 56.1 %copy-start.1 = (bf16[2,128,128]{2,1,0:T(8,128)(2,1)S(1)}, bf16[2,128,128]{2,1,0:T(8,128)(2,1)}, u32[]{:S(2)}) copy-start(bf16[2,128,128]{2,1,0:T(8,128)(2,1)} %param.11) | copy-start | bytes 196612
  7.2 56.1 %copy-start.2 = (bf16[2,128,128]{2,1,0:T(8,128)(2,1)S(1)}, bf16[2,128,128]{2,1,0:T(8,128)(2,1)}, u32[]{:S(2)}) copy-start(bf16[2,128,128]{2,1,0:T(8,128)(2,1)} %param.12) | copy-start | bytes 196612
  7.2 135.2 %all-gather.3.cloned.1.call-start = ((), (), s32[]{:S(2)}) async-start(), calls=%async_computation | async-start | bytes 2359296 | tf_op jit(solution)/shard_map/all_gather | solution.py:10
  8.1 53.7 %collective-permute-start.1 = (bf16[2,2,64,128]{3,2,1,0:T(8,128)(2,1)S(1)}, bf16[2,2,64,128]{3,2,1,0:T(8,128)(2,1)S(1)}, u32[]{:S(2)}, u32[]{:S(2)}) collective-permute-start(bf16[2,2,64,128]{3,2,1,0:T(8,128)(2,1)S(1)} %get-tuple-element.61), channel_id=1, source_target_pairs={{4,0},{8,4},{12,8},{16,12},{20,16},{24,20},{28,24},{5,1},{9,5},{13... | collective-permute-start | bytes 196616 | tf_op jit(solution)/shard_map/ppermute | solution.py:25
  9.4 52.5 %collective-permute-start = (bf16[2,2,64,128]{3,2,1,0:T(8,128)(2,1)S(1)}, bf16[2,2,64,128]{3,2,1,0:T(8,128)(2,1)S(1)}, u32[]{:S(2)}, u32[]{:S(2)}) collective-permute-start(bf16[2,2,64,128]{3,2,1,0:T(8,128)(2,1)S(1)} %get-tuple-element.60), channel_id=1, source_target_pairs={{0,4},{4,8},{8,12},{12,16},{16,20},{20,24},{24,28},{1,5},{5,9},{9,... | collective-permute-start | bytes 196616 | tf_op jit(solution)/shard_map/ppermute | solution.py:24
  15.8 47.4 %collective-permute-start.2 = (bf16[2,2,128,128]{3,2,1,0:T(8,128)(2,1)S(1)}, bf16[2,2,128,128]{3,2,1,0:T(8,128)(2,1)S(1)}, u32[]{:S(2)}, u32[]{:S(2)}) collective-permute-start(bf16[2,2,128,128]{3,2,1,0:T(8,128)(2,1)S(1)} %pad_maximum_fusion.7), channel_id=1, source_target_pairs={{0,4},{4,0},{8,12},{12,8},{16,20},{20,16},{24,28},{28,24},{1,5},{5... | collective-permute-start | bytes 393224 | tf_op jit(solution)/shard_map/ppermute | solution.py:33
  63.4 6.4 %collective-permute-start.7 = (bf16[2,2,128,128]{3,2,1,0:T(8,128)(2,1)S(1)}, bf16[2,2,128,128]{3,2,1,0:T(8,128)(2,1)S(1)}, u32[]{:S(2)}, u32[]{:S(2)}) collective-permute-start(bf16[2,2,128,128]{3,2,1,0:T(8,128)(2,1)S(1)} %get-tuple-element.53), channel_id=1, source_target_pairs={{0,8},{4,12},{8,0},{12,4},{16,24},{20,28},{24,16},{28,20},{1,9},{5... | collective-permute-start | bytes 393224 | tf_op jit(solution)/shard_map/ppermute | solution.py:33
  63.7 9.2 %collective-permute-start.5 = (bf16[2,2,128,128]{3,2,1,0:T(8,128)(2,1)S(1)}, bf16[2,2,128,128]{3,2,1,0:T(8,128)(2,1)S(1)}, u32[]{:S(2)}, u32[]{:S(2)}) collective-permute-start(bf16[2,2,128,128]{3,2,1,0:T(8,128)(2,1)S(1)} %get-tuple-element.54), channel_id=1, source_target_pairs={{0,8},{4,12},{8,0},{12,4},{16,24},{20,28},{24,16},{28,20},{1,9},{5... | collective-permute-start | bytes 393224 | tf_op jit(solution)/shard_map/ppermute | solution.py:33
  65.8 8.6 %collective-permute-start.3 = (bf16[2,2,128,128]{3,2,1,0:T(8,128)(2,1)S(1)}, bf16[2,2,128,128]{3,2,1,0:T(8,128)(2,1)S(1)}, u32[]{:S(2)}, u32[]{:S(2)}) collective-permute-start(bf16[2,2,128,128]{3,2,1,0:T(8,128)(2,1)S(1)} %get-tuple-element.52), channel_id=1, source_target_pairs={{0,8},{4,12},{8,0},{12,4},{16,24},{20,28},{24,16},{28,20},{1,9},{5... | collective-permute-start | bytes 393224 | tf_op jit(solution)/shard_map/ppermute | solution.py:33
  69.9 9.7 %collective-permute-start.8 = (bf16[2,2,128,128]{3,2,1,0:T(8,128)(2,1)S(1)}, bf16[2,2,128,128]{3,2,1,0:T(8,128)(2,1)S(1)}, u32[]{:S(2)}, u32[]{:S(2)}) collective-permute-start(bf16[2,2,128,128]{3,2,1,0:T(8,128)(2,1)S(1)} %broadcast_select_fusion.3), channel_id=1, source_target_pairs={{0,16},{4,20},{8,24},{12,28},{16,0},{20,4},{24,8},{28,12},{1,17},{... | collective-permute-start | bytes 393224 | tf_op jit(solution)/shard_map/ppermute | solution.py:33
  73.0 8.6 %collective-permute-start.6 = (bf16[2,2,128,128]{3,2,1,0:T(8,128)(2,1)S(1)}, bf16[2,2,128,128]{3,2,1,0:T(8,128)(2,1)S(1)}, u32[]{:S(2)}, u32[]{:S(2)}) collective-permute-start(bf16[2,2,128,128]{3,2,1,0:T(8,128)(2,1)S(1)} %broadcast_select_fusion.8), channel_id=1, source_target_pairs={{0,16},{4,20},{8,24},{12,28},{16,0},{20,4},{24,8},{28,12},{1,17},{... | collective-permute-start | bytes 393224 | tf_op jit(solution)/shard_map/ppermute | solution.py:33
  74.4 8.6 %collective-permute-start.4 = (bf16[2,2,128,128]{3,2,1,0:T(8,128)(2,1)S(1)}, bf16[2,2,128,128]{3,2,1,0:T(8,128)(2,1)S(1)}, u32[]{:S(2)}, u32[]{:S(2)}) collective-permute-start(bf16[2,2,128,128]{3,2,1,0:T(8,128)(2,1)S(1)} %broadcast_select_fusion.13), channel_id=1, source_target_pairs={{0,16},{4,20},{8,24},{12,28},{16,0},{20,4},{24,8},{28,12},{1,17},{... | collective-permute-start | bytes 393224 | tf_op jit(solution)/shard_map/ppermute | solution.py:33
  84.0 1.9 %copy-start.5 = (bf16[2,128,128]{2,1,0:T(8,128)(2,1)S(1)}, bf16[2,128,128]{2,1,0:T(8,128)(2,1)}, u32[]{:S(2)}) copy-start(bf16[2,128,128]{2,1,0:T(8,128)(2,1)} %param.13) | copy-start | bytes 196612
  85.3 1.6 %copy-start.3 = (bf16[1,2,2,8,64,128]{5,2,4,0,3,1:T(2,128)(2,1)}, bf16[1,2,2,8,64,128]{5,2,4,0,3,1:T(2,128)(2,1)S(1)}, u32[]{:S(2)}) copy-start(bf16[1,2,2,8,64,128]{5,2,4,0,3,1:T(2,128)(2,1)S(1)} %get-tuple-element.45) | copy-start | bytes 1572868
  88.5 6.4 %copy-start.4 = (bf16[1,2,2,8,64,128]{5,2,4,0,3,1:T(2,128)(2,1)S(1)}, bf16[1,2,2,8,64,128]{5,2,4,0,3,1:T(2,128)(2,1)}, u32[]{:S(2)}) copy-start(bf16[1,2,2,8,64,128]{5,2,4,0,3,1:T(2,128)(2,1)} %copy-done.3) | copy-start | bytes 1572868
  88.6 11.7 %collective-permute-start.10 = (bf16[2,2,64,128]{3,2,1,0:T(8,128)(2,1)S(1)}, bf16[2,2,64,128]{3,2,1,0:T(8,128)(2,1)S(1)}, u32[]{:S(2)}, u32[]{:S(2)}) collective-permute-start(bf16[2,2,64,128]{3,2,1,0:T(8,128)(2,1)S(1)} %get-tuple-element.51), channel_id=1, source_target_pairs={{4,0},{8,4},{12,8},{16,12},{20,16},{24,20},{28,24},{5,1},{9,5},{13... | collective-permute-start | bytes 196616 | tf_op jit(solution)/shard_map/ppermute | solution.py:25
  90.1 10.3 %collective-permute-start.9 = (bf16[2,2,64,128]{3,2,1,0:T(8,128)(2,1)S(1)}, bf16[2,2,64,128]{3,2,1,0:T(8,128)(2,1)S(1)}, u32[]{:S(2)}, u32[]{:S(2)}) collective-permute-start(bf16[2,2,64,128]{3,2,1,0:T(8,128)(2,1)S(1)} %get-tuple-element.50), channel_id=1, source_target_pairs={{0,4},{4,8},{8,12},{12,16},{16,20},{20,24},{24,28},{1,5},{5,9},{9,... | collective-permute-start | bytes 196616 | tf_op jit(solution)/shard_map/ppermute | solution.py:24
  98.1 5.4 %collective-permute-start.17 = (bf16[2,2,128,128]{3,2,1,0:T(8,128)(2,1)S(1)}, bf16[2,2,128,128]{3,2,1,0:T(8,128)(2,1)S(1)}, u32[]{:S(2)}, u32[]{:S(2)}) collective-permute-start(bf16[2,2,128,128]{3,2,1,0:T(8,128)(2,1)S(1)} %bitcast.128), channel_id=1, source_target_pairs={{0,4},{4,0},{8,12},{12,8},{16,20},{20,16},{24,28},{28,24},{1,5},{5... | collective-permute-start | bytes 393224 | tf_op jit(solution)/shard_map/ppermute | solution.py:33
  98.2 6.3 %collective-permute-start.14 = (bf16[2,2,128,128]{3,2,1,0:T(8,128)(2,1)S(1)}, bf16[2,2,128,128]{3,2,1,0:T(8,128)(2,1)S(1)}, u32[]{:S(2)}, u32[]{:S(2)}) collective-permute-start(bf16[2,2,128,128]{3,2,1,0:T(8,128)(2,1)S(1)} %bitcast.126), channel_id=1, source_target_pairs={{0,4},{4,0},{8,12},{12,8},{16,20},{20,16},{24,28},{28,24},{1,5},{5... | collective-permute-start | bytes 393224 | tf_op jit(solution)/shard_map/ppermute | solution.py:33
  100.3 5.6 %collective-permute-start.11 = (bf16[2,2,128,128]{3,2,1,0:T(8,128)(2,1)S(1)}, bf16[2,2,128,128]{3,2,1,0:T(8,128)(2,1)S(1)}, u32[]{:S(2)}, u32[]{:S(2)}) collective-permute-start(bf16[2,2,128,128]{3,2,1,0:T(8,128)(2,1)S(1)} %bitcast.124), channel_id=1, source_target_pairs={{0,4},{4,0},{8,12},{12,8},{16,20},{20,16},{24,28},{28,24},{1,5},{5... | collective-permute-start | bytes 393224 | tf_op jit(solution)/shard_map/ppermute | solution.py:33
  103.5 8.6 %collective-permute-start.18 = (bf16[2,2,128,128]{3,2,1,0:T(8,128)(2,1)S(1)}, bf16[2,2,128,128]{3,2,1,0:T(8,128)(2,1)S(1)}, u32[]{:S(2)}, u32[]{:S(2)}) collective-permute-start(bf16[2,2,128,128]{3,2,1,0:T(8,128)(2,1)S(1)} %broadcast_select_fusion), channel_id=1, source_target_pairs={{0,8},{4,12},{8,0},{12,4},{16,24},{20,28},{24,16},{28,20},{1,9},{5... | collective-permute-start | bytes 393224 | tf_op jit(solution)/shard_map/ppermute | solution.py:33
  104.6 11.2 %collective-permute-start.15 = (bf16[2,2,128,128]{3,2,1,0:T(8,128)(2,1)S(1)}, bf16[2,2,128,128]{3,2,1,0:T(8,128)(2,1)S(1)}, u32[]{:S(2)}, u32[]{:S(2)}) collective-permute-start(bf16[2,2,128,128]{3,2,1,0:T(8,128)(2,1)S(1)} %broadcast_select_fusion.5), channel_id=1, source_target_pairs={{0,8},{4,12},{8,0},{12,4},{16,24},{20,28},{24,16},{28,20},{1,9},{5... | collective-permute-start | bytes 393224 | tf_op jit(solution)/shard_map/ppermute | solution.py:33
  106.0 12.6 %collective-permute-start.12 = (bf16[2,2,128,128]{3,2,1,0:T(8,128)(2,1)S(1)}, bf16[2,2,128,128]{3,2,1,0:T(8,128)(2,1)S(1)}, u32[]{:S(2)}, u32[]{:S(2)}) collective-permute-start(bf16[2,2,128,128]{3,2,1,0:T(8,128)(2,1)S(1)} %broadcast_select_fusion.10), channel_id=1, source_target_pairs={{0,8},{4,12},{8,0},{12,4},{16,24},{20,28},{24,16},{28,20},{1,9},{5... | collective-permute-start | bytes 393224 | tf_op jit(solution)/shard_map/ppermute | solution.py:33
  112.2 6.8 %collective-permute-start.19 = (bf16[2,2,128,128]{3,2,1,0:T(8,128)(2,1)S(1)}, bf16[2,2,128,128]{3,2,1,0:T(8,128)(2,1)S(1)}, u32[]{:S(2)}, u32[]{:S(2)}) collective-permute-start(bf16[2,2,128,128]{3,2,1,0:T(8,128)(2,1)S(1)} %broadcast_select_fusion.2), channel_id=1, source_target_pairs={{0,16},{4,20},{8,24},{12,28},{16,0},{20,4},{24,8},{28,12},{1,17},{... | collective-permute-start | bytes 393224 | tf_op jit(solution)/shard_map/ppermute | solution.py:33
  115.9 14.5 %collective-permute-start.16 = (bf16[2,2,128,128]{3,2,1,0:T(8,128)(2,1)S(1)}, bf16[2,2,128,128]{3,2,1,0:T(8,128)(2,1)S(1)}, u32[]{:S(2)}, u32[]{:S(2)}) collective-permute-start(bf16[2,2,128,128]{3,2,1,0:T(8,128)(2,1)S(1)} %broadcast_select_fusion.7), channel_id=1, source_target_pairs={{0,16},{4,20},{8,24},{12,28},{16,0},{20,4},{24,8},{28,12},{1,17},{... | collective-permute-start | bytes 393224 | tf_op jit(solution)/shard_map/ppermute | solution.py:33
  118.7 18.6 %collective-permute-start.13 = (bf16[2,2,128,128]{3,2,1,0:T(8,128)(2,1)S(1)}, bf16[2,2,128,128]{3,2,1,0:T(8,128)(2,1)S(1)}, u32[]{:S(2)}, u32[]{:S(2)}) collective-permute-start(bf16[2,2,128,128]{3,2,1,0:T(8,128)(2,1)S(1)} %broadcast_select_fusion.12), channel_id=1, source_target_pairs={{0,16},{4,20},{8,24},{12,28},{16,0},{20,4},{24,8},{28,12},{1,17},{... | collective-permute-start | bytes 393224 | tf_op jit(solution)/shard_map/ppermute | solution.py:33
Sparse Core Ops, SparseCore 0:
  88.6 53.6 all-gather.2
